TPU v7x, 32 devices: a whole 2x2x4 slice. The times are simulated.
32 devices in a mesh: wide: 8 (over y, x, core), narrow: 4 (over z).
Axes of the slice: x: 2, y: 2, z: 4, core: 2. Of those that a mesh axis runs over, the one named last changes fastest.
Arguments:
- batch_index: int32 [256], P('narrow'), may hold values from 0 to 255
- train_features: float32 [1024, 1024], P('narrow'), may hold values from -6 to 6
- train_labels: float32 [1024, 1000], P('narrow'), may hold values from -12 to 12
- centers: float32 [8192, 1024], P(('wide', 'narrow')), may hold values from -6 to 6
- weights: float32 [8192, 1000], P(('wide', 'narrow')), may hold values from -6 to 6
Outputs:
- new_weights: float32 [8192, 1000], P(('wide', 'narrow'))
- residual: float32 [256, 1000], P('narrow')
Inputs may be any that keep to these rules, and one draw needn't show every extreme that they name: `batch_index`: entry i names a row of the training shard held by narrow index i // 64.
All inputs are finite; a program needn't handle non-finite values.
Results may differ from a plain program's by a relative error of at most 0.0001.
Values sent between devices are 32-bit elements; how exact they have to be, the bound alone decides.
A program may use at most 64 MiB of HBM per device.

v0:
```python
import functools
import math

import jax
import jax.numpy as jnp
from jax import lax
from jax.experimental import pallas as pl
from jax.experimental.pallas import tpu as pltpu
from jax.sharding import PartitionSpec as P

step_size = 1.0
MESH = pl.DeviceIdType.MESH
HIGHEST = lax.Precision.HIGHEST
ROW_DEPTH = 2
SUB = 8


def dot(a, b, dims):
    return lax.dot_general(
        a, b, (dims, ((), ())), precision=HIGHEST, preferred_element_type=jnp.float32
    )


def split(x, count):
    terms = []
    for _ in range(count):
        terms.append(x.astype(jnp.bfloat16))
        x = x - terms[-1].astype(jnp.float32)
    return terms


def split_dot(a, b):
    held = a[0].shape[0]
    orders = [[] for _ in a]
    for i, right in enumerate(b):
        left = a[: len(a) - i]
        out = lax.dot_general(
            jnp.concatenate(left, axis=0), right, (((1,), (1,)), ((), ())),
            preferred_element_type=jnp.float32,
        )
        for j in range(len(left)):
            orders[i + j].append(out[j * held : (j + 1) * held])
    total = 0.0
    for terms in orders[::-1]:
        total = total + sum(terms)
    return total


def plan(wide, block):
    stages, rows = [], block
    for _ in range(wide.bit_length() - 1):
        halves = rows >= 2 * SUB
        rows = rows // 2 if halves else rows
        stages.append((rows, halves))
    return stages


def step_kernel(
    wide, narrow, count, index_ref, tf_hbm, lab_hbm, cen_hbm, wgt_hbm, kern_hbm, all_hbm, res_hbm,
    tf, lab, cen, wgt, cen_terms, wgt_terms, rows, kern, away, part, resid, tgt, got, zgot, load_sem,
    zrow_s, zrow_r, row_s, row_r, pair_s, pair_r, kern_s, kern_r, red_s, red_r, zred_s, zred_r, zag_s, zag_r, ag_s, ag_r, out_sem,
):
    w, n = lax.axis_index("wide"), lax.axis_index("narrow")
    block = index_ref.shape[0]
    batch = block * narrow
    features, owned = cen.shape[2], cen.shape[1]
    stages = plan(wide, block)
    nst = len(stages)
    core = w % 2
    partner = (w + 1 - 2 * core, n)
    up = [2**k for k in range(1, nst)]
    masks = [1] + [jnp.where(core == 0, p, q) for p, q in zip(up, up[::-1])]
    side = [core] + [(w // m) % 2 for m in masks[1:]]
    peer = [partner] + [(w + m * (1 - 2 * s), n) for m, s in zip(masks[1:], side[1:])]
    start = [0]
    for s, (held, halves) in zip(side, stages):
        start.append(start[-1] + (s * held if halves else 0))
    start = [0] + [pl.multiple_of(s, SUB) for s in start[1:]]
    half = stages[0][0]

    loads = [
        pltpu.make_async_copy(src, dst, load_sem.at[i])
        for i, (src, dst) in enumerate(((tf_hbm, tf), (cen_hbm, cen.at[0]), (wgt_hbm, wgt.at[0]), (lab_hbm, lab)))
    ]
    for load in loads:
        load.start()
    zpeers = [(w, lax.rem(n + k, narrow)) for k in range(1, narrow)]
    barrier = pltpu.get_barrier_semaphore()
    for p in zpeers + peer:
        pl.semaphore_signal(barrier, inc=1, device_id=p, device_id_type=MESH)

    def copy(src, dst, ssem, rsem, to):
        return pltpu.make_async_remote_copy(
            src_ref=src, dst_ref=dst, send_sem=ssem, recv_sem=rsem, device_id=to, device_id_type=MESH
        )

    sent = []

    def send(*args, later=True):
        c = copy(*args)
        c.start()
        if later:
            sent.append(c)
        return c

    loads[0].wait()
    for g in range(block // SUB):
        picked = [tf[pl.ds(index_ref[g * SUB + i], 1), :] for i in range(SUB)]
        rows[n, pl.ds(g * SUB, SUB), :] = jnp.concatenate(picked, axis=0)
    pl.semaphore_wait(barrier, len(zpeers) + nst)

    def at(k):
        return lax.rem(n + k, narrow)

    def piece_of(j):
        held = stages[j][0]
        theirs = pl.multiple_of(start[j] + (1 - side[j]) * held, SUB)
        return pl.ds(start[j + 1], held), pl.ds(theirs, held)

    def spread(ref, zsem, sem, back, i, k):
        m = at(k)
        if i == 0:
            if k > 0:
                held = piece_of(back[0])[0]
                copy(ref.at[m, held], ref.at[m, held], zsem[0].at[k], zsem[1].at[k], partner).wait_recv()
        else:
            j = back[i - 1]
            theirs = piece_of(j)[1]
            copy(ref.at[m, theirs], ref.at[m, theirs], sem[0].at[j, k], sem[1].at[j, k], peer[j]).wait_recv()
        if i < len(back) and not (i == len(back) - 1 and back[i] == 0 and ref is rows):
            j = back[i]
            held = piece_of(j)[0]
            send(ref.at[m, held], ref.at[m, held], sem[0].at[j, k], sem[1].at[j, k], peer[j])

    def along_narrow(ref, held, zsem):
        for k in range(1, narrow):
            to = (w, lax.rem(n + narrow - k, narrow))
            send(ref.at[n, held], ref.at[n, held], zsem[0].at[k], zsem[1].at[k], to)

    cuts = [j for j in range(nst) if stages[j][1]][::-1]
    row_cuts = [j for j in cuts if j < ROW_DEPTH]
    mine, other = piece_of(0)
    along_narrow(rows, piece_of(row_cuts[0])[0], (zrow_s, zrow_r))

    loads[1].wait()
    send(cen.at[0], cen.at[1], pair_s.at[0], pair_r.at[0], partner)
    loads[2].wait()
    send(wgt.at[0], wgt.at[1], pair_s.at[1], pair_r.at[1], partner)
    ones = jnp.ones((SUB, features), jnp.float32)

    def squares(o):
        centers = cen[o]
        for i, term in enumerate(split(centers, 3)):
            cen_terms[o, i] = term
        return dot(ones, centers * centers, ((1,), (1,)))[0:1, :]

    center_sq = [squares(0)]

    def reduce_copy(j, k):
        m = at(k)
        held, halves = stages[j]
        first = start[j] + (1 - side[j]) * held if halves else start[j + 1]
        first = pl.multiple_of(first - core * half, SUB)
        return (
            part.at[m, pl.ds(first, held)], got[j - 1].at[k], red_s.at[j, k], red_r.at[j, k], peer[j]
        )

    sends = {}

    def begin(ks):
        piece = jnp.concatenate([rows[at(k), mine, :] for k in ks], axis=0)
        piece_sq = jnp.sum(piece * piece, axis=1, keepdims=True)
        piece_terms = split(piece, 3)
        total = 0.0
        for o in range(2):
            if len(center_sq) == o:
                copy(cen.at[0], cen.at[1], pair_s.at[0], pair_r.at[0], partner).wait_recv()
                center_sq.append(squares(o))
            inner = split_dot(piece_terms, [cen_terms[o, i] for i in range(3)])
            value = jnp.exp((2.0 * features - piece_sq - center_sq[o] + 2.0 * inner) / 128.0)
            for i, k in enumerate(ks):
                this = value[i * half : (i + 1) * half, :]
                if o == 0:
                    kern[at(k), mine, :] = this
                else:
                    away[k] = this
            if o == 1 and 0 in ks:
                copy(wgt.at[0], wgt.at[1], pair_s.at[1], pair_r.at[1], partner).wait_recv()
            if 0 in ks:
                for i, term in enumerate(split(wgt[o], 2)):
                    wgt_terms[o, i] = term
            total = total + split_dot(split(value, 2), [wgt_terms[o, i] for i in range(2)])
        for i, k in enumerate(ks):
            part[at(k)] = total[i * half : (i + 1) * half, :]
        for k in ks:
            sends[1, k] = send(*reduce_copy(1, k), later=stages[1][1])
        for k in ks:
            send(away.at[k], kern.at[at(k), mine], kern_s.at[k], kern_r.at[k], partner)

    def reduce(j, k):
        m = at(k)
        held, halves = stages[j]
        copy(*reduce_copy(j, k)).wait_recv()
        if not halves:
            sends[j, k].wait_send()
        keep = pl.ds(pl.multiple_of(start[j + 1] - core * half, SUB), held)
        part[m, keep, :] = part[m, keep, :] + got[j - 1][k]
        if j + 1 < nst:
            sends[j + 1, k] = send(*reduce_copy(j + 1, k), later=stages[j + 1][1])
        elif k > 0:
            send(part.at[m, keep], zgot.at[k], zred_s.at[k], zred_r.at[k], (w, m))

    begin([0])
    for i in range(len(row_cuts)):
        for k in range(1, narrow):
            spread(rows, (zrow_s, zrow_r), (row_s, row_r), row_cuts, i, k)
        if i + 1 < nst:
            reduce(i + 1, 0)
    for i in range(len(row_cuts) + 1, nst):
        reduce(i, 0)
    begin(list(range(1, narrow)))
    for j in range(1, nst):
        for k in range(1, narrow):
            reduce(j, k)

    last = stages[-1][0]
    keep = pl.ds(start[nst], last)
    loads[3].wait()
    column = lax.broadcasted_iota(jnp.int32, (1, lab.shape[1]), 1)
    chosen = [jnp.where(column == index_ref[start[nst] + i], 1.0, 0.0) for i in range(last)]
    tgt[...] = dot(jnp.concatenate(chosen, axis=0), lab[...], ((1,), (1,)))
    own = pl.ds(pl.multiple_of(start[nst] - core * half, SUB), last)
    total = part[n, own, :]
    for k in range(1, narrow):
        copy(part.at[n, own], zgot.at[k], zred_s.at[k], zred_r.at[k], partner).wait_recv()
        total = total + zgot[k]
    resid[n, keep, :] = total * (1.0 / math.sqrt(count)) - tgt[...]

    along_narrow(resid, keep, (zag_s, zag_r))
    for k in range(narrow):
        copy(away.at[k], kern.at[at(k), other], kern_s.at[k], kern_r.at[k], partner).wait_recv()
    outs = [pltpu.make_async_copy(kern, kern_hbm, out_sem.at[0])]
    outs[0].start()
    tail = len(cuts)
    order = [(0, 0), (1, 0)] if tail else [(0, 0)]
    for i in range(tail + 1):
        order += [(i, k) for k in range(1, narrow)]
        order += [(i + 2, 0)] if i + 2 <= tail else []
    for i, k in order:
        spread(resid, (zag_s, zag_r), (ag_s, ag_r), cuts, i, k)
        if i == tail:
            m = at(k)
            outs.append(pltpu.make_async_copy(resid.at[m], all_hbm.at[m], out_sem.at[1 + k]))
            outs[-1].start()
            if k == 0:
                outs.append(pltpu.make_async_copy(resid.at[n], res_hbm, out_sem.at[1 + narrow]))
                outs[-1].start()
    for c in sent:
        c.wait_send()
    for c in outs:
        c.wait()


def per_device(batch_index, train_features, train_labels, centers, weights):
    wide, narrow = lax.axis_size("wide"), lax.axis_size("narrow")
    block, features = batch_index.shape[0], centers.shape[1]
    outputs, owned = weights.shape[1], centers.shape[0]
    labels_t, weights_t = train_labels.T, weights.T
    stages = plan(wide, block)
    nst, last = len(stages), stages[-1][0]
    f32, dma = jnp.float32, pltpu.SemaphoreType.DMA
    anywhere = pl.BlockSpec(memory_space=pl.ANY)
    kernel, every, residual = pl.pallas_call(
        functools.partial(step_kernel, wide, narrow, owned * wide * narrow),
        out_shape=(
            jax.ShapeDtypeStruct((narrow, block, owned), f32),
            jax.ShapeDtypeStruct((narrow, block, outputs), f32),
            jax.ShapeDtypeStruct((block, outputs), f32),
        ),
        in_specs=[pl.BlockSpec(memory_space=pltpu.SMEM)] + [anywhere] * 4,
        out_specs=(anywhere, anywhere, anywhere),
        scratch_shapes=[
            pltpu.VMEM(train_features.shape, f32),
            pltpu.VMEM(labels_t.shape, f32),
            pltpu.VMEM((2, *centers.shape), f32),
            pltpu.VMEM((2, *weights_t.shape), f32),
            pltpu.VMEM((2, 3, *centers.shape), jnp.bfloat16),
            pltpu.VMEM((2, 2, *weights_t.shape), jnp.bfloat16),
            pltpu.VMEM((narrow, block, features), f32),
            pltpu.VMEM((narrow, block, owned), f32),
            pltpu.VMEM((narrow, block // 2, owned), f32),
            pltpu.VMEM((narrow, block // 2, outputs), f32),
            pltpu.VMEM((narrow, block, outputs), f32),
            pltpu.VMEM((last, outputs), f32),
            [pltpu.VMEM((narrow, held, outputs), f32) for held, _ in stages[1:]],
            pltpu.VMEM((narrow, last, outputs), f32),
            dma((4,)),
            dma((narrow,)), dma((narrow,)),
            dma((nst, narrow)), dma((nst, narrow)),
            dma((2,)), dma((2,)),
            dma((narrow,)), dma((narrow,)),
            dma((nst, narrow)), dma((nst, narrow)),
            dma((narrow,)), dma((narrow,)),
            dma((narrow,)), dma((narrow,)),
            dma((nst, narrow)), dma((nst, narrow)),
            dma((2 + narrow,)),
        ],
        compiler_params=pltpu.CompilerParams(
            collective_id=0, has_side_effects=True, vmem_limit_bytes=60 * 2**20
        ),
    )(batch_index, train_features, labels_t, centers, weights_t)
    batch = narrow * block
    delta = lax.dot_general(
        kernel.reshape(batch, owned), every.reshape(batch, outputs), (((0,), (0,)), ((), ())),
        precision=lax.Precision.HIGH, preferred_element_type=f32,
    )
    return weights - step_size / batch * delta, residual


def solution(mesh):
    in_specs = (
        P("narrow"),
        P("narrow", None),
        P("narrow", None),
        P(("wide", "narrow"), None),
        P(("wide", "narrow"), None),
    )
    out_specs = (P(("wide", "narrow"), None), P("narrow", None))
    return jax.shard_map(
        per_device, mesh=mesh, in_specs=in_specs, out_specs=out_specs, check_vma=False
    )
```

profile of v0, /device:TPU:0, one launch (start us, length us, event | category | flops | bytes accessed | tf_op | source)
XLA Modules:
  0.0 49.9 jit_solution(6450379479462925770)
XLA Ops:
  0.6 0.0 copy-start
  0.6 45.2 %shard_map.68 = (f32[4,64,256]{2,1,0:T(8,128)}, f32[4,64,1000]{2,1,0:T(8,128)}, f32[64,1000]{1,0:T(8,128)}) custom-call(s32[64]{0:T(128)} %index_ref.1, f32[256,1024]{1,0:T(8,128)} %tf_hbm.1, f32[1000,256]{1,0:T(8,128)} %bitcast.11, f32[256,1024]{1,0:T(8,128)} %cen_hbm.1, f32[1000,256]{1,0:T(8,128)} %bitcast.10), custom_call_target="tpu_custom_call" | custom-call | tf_op jit(solution)/shard_map/pallas_call | solution.py:273
  45.8 0.0 copy-done
  45.8 0.0 copy-start.1
  45.9 3.3 %fusion.1 = f32[256,1000]{0,1:T(8,128)} fusion(f32[256,1000]{0,1:T(8,128)S(1)} %copy-done, f32[4,64,256]{2,1,0:T(8,128)} %get-tuple-element.5, f32[4,64,1000]{2,1,0:T(8,128)} %get-tuple-element.6), kind=kOutput, calls=%fused_computation.2 | convolution fusion | flops 393728000 | bytes 3334144 | tf_op jit(solution)/shard_map/dot_general | solution.py:313
  49.2 0.0 copy-done.1
  49.2 0.7 %copy.8 = f32[64,1000]{1,0:T(8,128)} copy(f32[64,1000]{1,0:T(8,128)S(1)} %copy-done.1) | data formatting | bytes 512000
Async XLA Ops:
  0.6 45.2 %copy-start = (f32[256,1000]{0,1:T(8,128)S(1)}, f32[256,1000]{0,1:T(8,128)}, u32[]{:S(2)}) copy-start(f32[256,1000]{0,1:T(8,128)} %param.9) | copy-start | bytes 3072004
  45.8 3.3 %copy-start.1 = (f32[64,1000]{1,0:T(8,128)S(1)}, f32[64,1000]{1,0:T(8,128)}, u32[]{:S(2)}) copy-start(f32[64,1000]{1,0:T(8,128)} %get-tuple-element.11) | copy-start | bytes 768004
where the time goes:
time: 50.6 us; the launch traced here: 49.9 us
  Pallas kernels  45.2 us (89%)
  matrix products  3.31 us (7%)
  local copies, waits for them, and re-layouts  0.71 us (1%)
  between operations  0.66 us (1%)
    pallas_call x1, Pallas kernels, per_device(): pl.pallas_call(functools.partial(step_kernel, wide, narrow, owned * wide...  45.2 us
    dot_general x1, matrix products, per_device(): lax.dot_general(kernel.reshape(batch, owned), every.reshape(batch, output...  3.31 us

commit v1 on v0

v1 whole, which is shorter than its diff:
```python
import functools
import math

import jax
import jax.numpy as jnp
from jax import lax
from jax.experimental import pallas as pl
from jax.experimental.pallas import tpu as pltpu
from jax.sharding import PartitionSpec as P

step_size = 1.0
MESH = pl.DeviceIdType.MESH
HIGHEST = lax.Precision.HIGHEST
SUB = 8
LANES = 128


def dot(a, b, dims):
    return lax.dot_general(
        a, b, (dims, ((), ())), precision=HIGHEST, preferred_element_type=jnp.float32
    )


def split(x, count):
    terms = []
    for _ in range(count):
        terms.append(x.astype(jnp.bfloat16))
        x = x - terms[-1].astype(jnp.float32)
    return terms


def split_dot(a, b):
    held = a[0].shape[0]
    orders = [[] for _ in a]
    for i, right in enumerate(b):
        left = a[: len(a) - i]
        out = lax.dot_general(
            jnp.concatenate(left, axis=0), right, (((1,), (1,)), ((), ())),
            preferred_element_type=jnp.float32,
        )
        for j in range(len(left)):
            orders[i + j].append(out[j * held : (j + 1) * held])
    total = 0.0
    for terms in orders[::-1]:
        total = total + sum(terms)
    return total


def flip(q, k):
    out = q
    for b in range(k.bit_length()):
        if k >> b & 1:
            out = out + 2**b * (1 - 2 * ((q // 2**b) % 2))
    return out


def by_distance(n, narrow):
    picks = []
    for p in range(1, narrow):
        m = 0
        for i in range(narrow):
            near = sorted(range(narrow), key=lambda j: abs(j - i))
            m = m + jnp.where(n == i, near[p], 0)
        picks.append(m)
    return picks


def step_kernel(
    wide, narrow, count, index_ref, tf_hbm, lab_hbm, cen_hbm, wgt_hbm, delta_hbm, res_hbm,
    tf, lab, cen, wgt, cen_terms, wgt_terms, rows, kern, away, part, got, zgot, resid, tgt, acc, load_sem,
    zrow_s, zrow_r, row_s, row_r, pair_s, pair_r, kern_s, kern_r, red_s, red_r, zred_s, zred_r,
    zag_s, zag_r, ag_s, ag_r, core_s, core_r, out_sem,
):
    w, n = lax.axis_index("wide"), lax.axis_index("narrow")
    plane = wide // 2
    c, q = w % 2, w // 2
    piece, features = rows.shape[2], rows.shape[3]
    half, outputs = plane * piece, acc.shape[0]
    partner = (w + 1 - 2 * c, n)
    hops = list(range(plane - 1, 0, -1))
    peer = {k: (flip(q, k) * 2 + c, n) for k in hops}
    others = by_distance(n, narrow)

    loads = [
        pltpu.make_async_copy(src, dst, load_sem.at[i])
        for i, (src, dst) in enumerate(((tf_hbm, tf), (cen_hbm, cen.at[0]), (wgt_hbm, wgt.at[0]), (lab_hbm, lab)))
    ]
    for load in loads:
        load.start()
    barrier = pltpu.get_barrier_semaphore()
    greeted = [(w, m) for m in others] + [peer[k] for k in hops] + [partner]
    for p in greeted:
        pl.semaphore_signal(barrier, inc=1, device_id=p, device_id_type=MESH)

    def copy(src, dst, ssem, rsem, to):
        return pltpu.make_async_remote_copy(
            src_ref=src, dst_ref=dst, send_sem=ssem, recv_sem=rsem, device_id=to, device_id_type=MESH
        )

    sent = []

    def send(*args):
        sent.append(copy(*args))
        sent[-1].start()

    loads[0].wait()
    first = c * half
    for g in range(plane):
        picked = [tf[pl.ds(index_ref[first + g * piece + i], 1), :] for i in range(piece)]
        rows[n, g] = jnp.concatenate(picked, axis=0)
    pl.semaphore_wait(barrier, len(greeted))

    for m in others:
        send(rows.at[n, q], rows.at[n, q], zrow_s.at[m], zrow_r.at[n], (w, m))
    loads[1].wait()
    send(cen.at[0], cen.at[1], pair_s.at[0], pair_r.at[0], partner)
    loads[2].wait()
    send(wgt.at[0], wgt.at[1], pair_s.at[1], pair_r.at[1], partner)

    def squares(o):
        centers = cen[o]
        for i, term in enumerate(split(centers, 3)):
            cen_terms[o, i] = term
        sq = centers * centers
        narrowed = sum(sq[:, j * LANES : (j + 1) * LANES] for j in range(features // LANES))
        return dot(jnp.ones((SUB, LANES), jnp.float32), narrowed, ((1,), (1,)))[0:1, :]

    def weigh(o):
        for i, term in enumerate(split(wgt[o], 2)):
            wgt_terms[o, i] = term

    def spread_rows(m):
        copy(rows.at[m, q], rows.at[m, q], zrow_s.at[m], zrow_r.at[m], partner).wait_recv()
        for k in hops:
            send(rows.at[m, q], rows.at[m, q], row_s.at[k, m], row_r.at[k, m], peer[k])

    center_sq = []

    def kernels(m, o, terms, sq):
        inner = split_dot(terms, [cen_terms[o, i] for i in range(3)])
        return jnp.exp((2.0 * features - sq - center_sq[o] + 2.0 * inner) / 128.0)

    def block_rows(m):
        mine = rows[m].reshape(half, features)
        return split(mine, 3), jnp.sum(mine * mine, axis=1, keepdims=True)

    def predict(o, value):
        return split_dot(split(value, 2), [wgt_terms[o, i] for i in range(2)])

    def reduce_send(m, total):
        part[m] = total.reshape(plane, piece, outputs)
        for k in hops:
            send(part.at[m, flip(q, k)], got.at[k, m], red_s.at[k, m], red_r.at[k, m], peer[k])
        send(away.at[m], kern.at[m, c], kern_s.at[m], kern_r.at[m], partner)

    def finish(m, terms, sq):
        value = kernels(m, 0, terms, sq)
        kern[m, c] = value
        total = predict(0, value)
        value = kernels(m, 1, terms, sq)
        away[m] = value
        reduce_send(m, total + predict(1, value))

    terms, sq = block_rows(n)
    center_sq.append(squares(0))
    weigh(0)
    value = kernels(n, 0, terms, sq)
    kern[n, c] = value
    total = predict(0, value)
    spread_rows(others[0])
    copy(cen.at[0], cen.at[1], pair_s.at[0], pair_r.at[0], partner).wait_recv()
    center_sq.append(squares(1))
    for m in others[1:]:
        spread_rows(m)
    copy(wgt.at[0], wgt.at[1], pair_s.at[1], pair_r.at[1], partner).wait_recv()
    weigh(1)
    value = kernels(n, 1, terms, sq)
    away[n] = value
    reduce_send(n, total + predict(1, value))

    loads[3].wait()
    own = first + q * piece
    column = lax.broadcasted_iota(jnp.int32, (1, lab.shape[1]), 1)
    chosen = [jnp.where(column == index_ref[own + i], 1.0, 0.0) for i in range(piece)]
    tgt[...] = dot(jnp.concatenate(chosen, axis=0), lab[...], ((1,), (1,)))

    def reduced(m):
        total = part[m, q]
        for k in hops[::-1]:
            copy(part.at[m, q], got.at[k, m], red_s.at[k, m], red_r.at[k, m], partner).wait_recv()
            total = total + got[k, m]
        return total

    def pass_on(m):
        part[m, q] = reduced(m)
        send(part.at[m, q], zgot.at[n], zred_s.at[m], zred_r.at[n], (w, m))

    for p, m in enumerate(others):
        for k in hops[::-1]:
            copy(rows.at[m, q], rows.at[m, flip(q, k)], row_s.at[k, m], row_r.at[k, m], partner).wait_recv()
        finish(m, *block_rows(m))
        if p > 0:
            pass_on(others[p - 1])
    total = reduced(n)
    pass_on(others[-1])
    for m in others:
        copy(part.at[m, q], zgot.at[m], zred_s.at[m], zred_r.at[m], partner).wait_recv()
        total = total + zgot[m]
    resid[n, c, q] = total * (1.0 / math.sqrt(count)) - tgt[...]

    def around(m):
        for k in hops:
            send(resid.at[m, c, q], resid.at[m, c, q], ag_s.at[k, m], ag_r.at[k, m], peer[k])

    for m in others:
        send(resid.at[n, c, q], resid.at[n, c, q], zag_s.at[m], zag_r.at[n], (w, m))
    around(n)

    def onward(m):
        copy(resid.at[m, c, q], resid.at[m, c, q], zag_s.at[m], zag_r.at[m], partner).wait_recv()
        around(m)

    def across(m):
        for k in hops[::-1]:
            there = resid.at[m, c, flip(q, k)]
            copy(there, there, ag_s.at[k, m], ag_r.at[k, m], partner).wait_recv()
        send(resid.at[m, c], resid.at[m, c], core_s.at[m], core_r.at[m], partner)

    def terms_of(m):
        copy(resid.at[m, c], resid.at[m, 1 - c], core_s.at[m], core_r.at[m], partner).wait_recv()
        copy(away.at[m], kern.at[m, 1 - c], kern_s.at[m], kern_r.at[m], partner).wait_recv()
        k_hi, k_lo = split(kern[m].reshape(2 * half, kern.shape[3]), 2)
        r_hi, r_lo = split(resid[m].reshape(2 * half, outputs), 2)
        return jnp.concatenate([r_hi, r_hi, r_lo], axis=0), jnp.concatenate([k_hi, k_lo, k_hi], axis=0)

    def contract(r, k):
        return lax.dot_general(r, k, (((0,), (0,)), ((), ())), preferred_element_type=jnp.float32)

    outs = [pltpu.make_async_copy(resid.at[n], res_hbm, out_sem.at[0])]
    order = [n] + others
    for p, m in enumerate(order):
        if p == 0:
            onward(others[0])
            across(n)
            for later in others[1:]:
                onward(later)
        else:
            across(m)
            before = order[p - 1]
            d = contract(*terms_of(before))
            acc[...] = d if p == 1 else acc[...] + d
            if p == 1:
                outs[0].start()
    r, k = terms_of(order[-1])
    cut = 2 * LANES
    for j, at in enumerate(range(0, outputs, cut)):
        span = pl.ds(at, min(cut, outputs - at))
        acc[span, :] = acc[span, :] + contract(r[:, at : at + cut], k)
        outs.append(pltpu.make_async_copy(acc.at[span], delta_hbm.at[span], out_sem.at[1 + j]))
        outs[-1].start()
    for s in sent:
        s.wait_send()
    for s in outs:
        s.wait()


def per_device(batch_index, train_features, train_labels, centers, weights):
    wide, narrow = lax.axis_size("wide"), lax.axis_size("narrow")
    block, features = batch_index.shape[0], centers.shape[1]
    outputs, owned = weights.shape[1], centers.shape[0]
    labels_t, weights_t = train_labels.T, weights.T
    plane, half = wide // 2, block // 2
    piece = half // plane
    f32, dma = jnp.float32, pltpu.SemaphoreType.DMA
    anywhere = pl.BlockSpec(memory_space=pl.ANY)
    each, pairs = dma((narrow,)), dma((plane, narrow))
    delta_t, residual = pl.pallas_call(
        functools.partial(step_kernel, wide, narrow, owned * wide * narrow),
        out_shape=(
            jax.ShapeDtypeStruct((outputs, owned), f32),
            jax.ShapeDtypeStruct((2, plane, piece, outputs), f32),
        ),
        in_specs=[pl.BlockSpec(memory_space=pltpu.SMEM)] + [anywhere] * 4,
        out_specs=(anywhere, anywhere),
        scratch_shapes=[
            pltpu.VMEM(train_features.shape, f32),
            pltpu.VMEM(labels_t.shape, f32),
            pltpu.VMEM((2, *centers.shape), f32),
            pltpu.VMEM((2, *weights_t.shape), f32),
            pltpu.VMEM((2, 3, *centers.shape), jnp.bfloat16),
            pltpu.VMEM((2, 2, *weights_t.shape), jnp.bfloat16),
            pltpu.VMEM((narrow, plane, piece, features), f32),
            pltpu.VMEM((narrow, 2, half, owned), f32),
            pltpu.VMEM((narrow, half, owned), f32),
            pltpu.VMEM((narrow, plane, piece, outputs), f32),
            pltpu.VMEM((plane, narrow, piece, outputs), f32),
            pltpu.VMEM((narrow, piece, outputs), f32),
            pltpu.VMEM((narrow, 2, plane, piece, outputs), f32),
            pltpu.VMEM((piece, outputs), f32),
            pltpu.VMEM((outputs, owned), f32),
            dma((4,)),
            each, each, pairs, pairs,
            dma((2,)), dma((2,)),
            each, each, pairs, pairs,
            each, each,
            each, each, pairs, pairs,
            each, each,
            dma((2 + outputs // (2 * LANES),)),
        ],
        compiler_params=pltpu.CompilerParams(
            collective_id=0, has_side_effects=True, vmem_limit_bytes=60 * 2**20
        ),
    )(batch_index, train_features, labels_t, centers, weights_t)
    new_weights = weights - step_size / (narrow * block) * delta_t.T
    return new_weights, residual.reshape(block, outputs)


def solution(mesh):
    in_specs = (
        P("narrow"),
        P("narrow", None),
        P("narrow", None),
        P(("wide", "narrow"), None),
        P(("wide", "narrow"), None),
    )
    out_specs = (P(("wide", "narrow"), None), P("narrow", None))
    return jax.shard_map(
        per_device, mesh=mesh, in_specs=in_specs, out_specs=out_specs, check_vma=False
    )
```

time: 50.6 us -> 46.4 us (0.917)
  matrix products: 3.31 us -> 0 us
  Pallas kernels: 45.2 us -> 42.1 us
  other arithmetic: 0 us -> 2.35 us
    dot_general x1 -> x0, matrix products: 3.31 us -> none  [per_device(): lax.dot_general(kernel.reshape(batch, owned), every.reshape(batch, output...]
    pallas_call x1, Pallas kernels: 45.2 us -> 42.1 us  [per_device(): pl.pallas_call(functools.partial(step_kernel, wide, narrow, owned * wide...]
    sub x0 -> x1, other arithmetic: none -> 2.35 us  [per_device(): new_weights = weights - step_size / (narrow * block) * delta_t.T]
where the time goes in v1:
time: 46.4 us; the launch traced here: 45.8 us
  Pallas kernels  42.1 us (91%)
  other arithmetic  2.35 us (5%)
  local copies, waits for them, and re-layouts  0.71 us (2%)
  between operations  0.66 us (1%)
    pallas_call x1, Pallas kernels, per_device(): pl.pallas_call(functools.partial(step_kernel, wide, narrow, owned * wide...  42.1 us
    sub x1, other arithmetic, per_device(): new_weights = weights - step_size / (narrow * block) * delta_t.T  2.35 us

profile of v1, /device:TPU:0, one launch (start us, length us, event | category | flops | bytes accessed | tf_op | source)
XLA Modules:
  0.0 45.8 jit_solution(8000544437858059037)
XLA Ops:
  0.6 0.0 copy-start
  0.6 42.1 %shard_map.68 = (f32[1000,256]{1,0:T(8,128)}, f32[2,4,8,1000]{3,2,1,0:T(8,128)}) custom-call(s32[64]{0:T(128)} %index_ref.1, f32[256,1024]{1,0:T(8,128)} %tf_hbm.1, f32[1000,256]{1,0:T(8,128)} %bitcast.6, f32[256,1024]{1,0:T(8,128)} %cen_hbm.1, f32[1000,256]{1,0:T(8,128)} %bitcast.5), custom_call_target="tpu_custom_call" | custom-call | tf_op jit(solution)/shard_map/pallas_call | solution.py:277
  42.8 0.0 copy-done
  42.8 0.0 copy-start.1
  42.8 2.3 %bitcast_subtract_fusion = f32[256,1000]{0,1:T(8,128)} fusion(f32[256,1000]{0,1:T(8,128)S(1)} %copy-done, f32[1000,256]{1,0:T(8,128)} %get-tuple-element.4), kind=kLoop, calls=%fused_computation | loop fusion | flops 512000 | bytes 3072000 | tf_op jit(solution)/shard_map/sub | solution.py:314
  45.1 0.0 copy-done.1
  45.1 0.7 %copy.8 = f32[64,1000]{1,0:T(8,128)} copy(f32[64,1000]{1,0:T(8,128)S(1)} %bitcast.7) | data formatting | bytes 512000
Async XLA Ops:
  0.6 42.1 %copy-start = (f32[256,1000]{0,1:T(8,128)S(1)}, f32[256,1000]{0,1:T(8,128)}, u32[]{:S(2)}) copy-start(f32[256,1000]{0,1:T(8,128)} %param.9) | copy-start | bytes 3072004
  42.8 2.4 %copy-start.1 = (f32[2,4,8,1000]{3,2,1,0:T(8,128)S(1)}, f32[2,4,8,1000]{3,2,1,0:T(8,128)}, u32[]{:S(2)}) copy-start(f32[2,4,8,1000]{3,2,1,0:T(8,128)} %get-tuple-element.5) | copy-start | bytes 768004
